TPU v7x, 32 devices: a whole 2x2x4 slice. The times are simulated.
32 devices in a mesh: section: 2 (over x), dp: 4 (over y, core), tensor: 4 (over z).
Axes of the slice: x: 2, y: 2, z: 4, core: 2. Of those that a mesh axis runs over, the one named last changes fastest.
Arguments:
- inputs: bfloat16 [8, 1024, 1024], P('dp', 'tensor'), may hold values from -6 to 6
- out_cotangent: bfloat16 [8, 1024, 1024], P('dp', 'tensor'), may hold values from -6 to 6
- group_ids: int32 [8, 1024], P('dp', 'tensor'), may hold values from 0 to 7
- group_weights: float32 [8], replicated, may hold values from 0.25 to 4
- gains: float32 [2, 4, 1024], P('section'), may hold values from 0.1 to 1.9
- qkv_weight: bfloat16 [2, 1024, 3, 1024], P('section', None, None, 'tensor'), may hold values from -0.1875 to 0.1875
- out_weight: bfloat16 [2, 1024, 1024], P('section', 'tensor'), may hold values from -0.1875 to 0.1875
- up_weight: bfloat16 [2, 1024, 4096], P('section', None, 'tensor'), may hold values from -0.1875 to 0.1875
- down_weight: bfloat16 [2, 4096, 1024], P('section', 'tensor'), may hold values from -0.09375 to 0.09375
Outputs:
- layer_outputs: bfloat16 [2, 8, 1024, 1024], P('section', 'dp', 'tensor')
- input_grads: bfloat16 [2, 8, 1024, 1024], P('section', 'dp', 'tensor')
- gains_grad: float32 [2, 4, 1024], P('section', None, ('dp', 'tensor'))
- qkv_grad: float32 [2, 1024, 3, 1024], P('section', 'dp', None, 'tensor')
- out_grad: float32 [2, 1024, 1024], P('section', 'tensor', 'dp')
- up_grad: float32 [2, 1024, 4096], P('section', 'dp', 'tensor')
- down_grad: float32 [2, 4096, 1024], P('section', 'tensor', 'dp')
All inputs are finite; a program needn't handle non-finite values.
Results may differ from a plain program's by a relative error of at most 0.02.
Values may be sent and summed in bfloat16 or wider, within the bound.
No kernel may reach another device: no remote copies, remote signals or barrier semaphores. Data moves between devices by JAX's collectives and lax.ppermute only.
A program may use at most 192 MiB of HBM per device.

v0:
```python
import jax
import jax.numpy as jnp
from jax import lax
from jax.sharding import PartitionSpec as P

HEAD_DIM = 64
NORM_EPSILON = 1e-06


def shifted(block, axis, distance):
    devices = range(lax.axis_size(axis))
    route = [(i - distance, i) for i in devices if i - distance in devices]
    return lax.ppermute(block, axis, route)


def norm_rows(vector, weight_gain):
    return (
        vector
        * lax.rsqrt(jnp.mean(vector * vector, axis=-1, keepdims=True) + NORM_EPSILON)
        * weight_gain
    )


def rotary_tables(seq_len, head_width):
    half_width = head_width // 2
    freqs = 10000.0 ** (-2.0 * jnp.arange(half_width, dtype=jnp.float32) / head_width)
    angles = jnp.arange(seq_len, dtype=jnp.float32)[:, None] * freqs[None, :]
    return (jnp.cos(angles), jnp.sin(angles))


def rotate(vector, cos_table, sin_table):
    first_half, second_half = jnp.split(vector, 2, axis=-1)
    cos_part = cos_table[:, None, :]
    sin_part = sin_table[:, None, :]
    return jnp.concatenate(
        [
            first_half * cos_part - second_half * sin_part,
            second_half * cos_part + first_half * sin_part,
        ],
        axis=-1,
    )


def contract(left_rows, right_rows):
    return lax.dot_general(
        left_rows, right_rows, (((0,), (0,)), ((), ())), preferred_element_type=jnp.float32
    )


def gather_rows(row_values, weight):

    def project(shard_rows, offset):
        return (shard_rows, jnp.dot(shard_rows, weight, preferred_element_type=jnp.float32))

    return project(lax.all_gather(row_values, "tensor", axis=0, tiled=True), jnp.int32(0))


def scatter_rows(row_values, weight, row_count):

    def partial_term(offset, span):
        return jnp.dot(row_values, weight, preferred_element_type=jnp.float32)

    return lax.psum_scatter(
        partial_term(jnp.int32(0), lax.axis_size("tensor") * row_count),
        "tensor",
        scatter_dimension=0,
        tiled=True,
    )


def gather_grads(row_values, weight):

    def project(shard_rows, offset):
        return (shard_rows, jnp.dot(shard_rows, weight.T, preferred_element_type=jnp.float32))

    return project(lax.all_gather(row_values, "tensor", axis=0, tiled=True), jnp.int32(0))


def scatter_grads(row_values, weight, row_count):

    def partial_term(offset, span):
        return jnp.dot(row_values, weight.T, preferred_element_type=jnp.float32)

    return lax.psum_scatter(
        partial_term(jnp.int32(0), lax.axis_size("tensor") * row_count),
        "tensor",
        scatter_dimension=0,
        tiled=True,
    )


def attention_probs(queries, key_rows):
    scores = jnp.einsum(
        "qhd,khd->hqk", queries, key_rows, preferred_element_type=jnp.float32
    ) * HEAD_DIM ** (-0.5)
    length = queries.shape[0]
    positions = jnp.arange(length, dtype=jnp.int32)
    causal = positions[:, None] >= positions[None, :]
    scores = jnp.where(causal[None], scores, -1e30)
    expos = jnp.exp(scores - jnp.max(scores, axis=-1, keepdims=True))
    return expos / jnp.sum(expos, axis=-1, keepdims=True)


def layer_forward(layer_input, weights):
    gains, w_qkv, w_out, w_up, w_down = weights
    row_count, model_width = layer_input.shape
    attn_in = norm_rows(layer_input, gains[0]).astype(jnp.bfloat16)
    gathered_a, qkv = gather_rows(attn_in, w_qkv.reshape(model_width, -1))
    length = qkv.shape[0]
    head_count = w_qkv.shape[2] // HEAD_DIM
    qkv = qkv.reshape(length, 3, head_count, HEAD_DIM)
    cos_table, sin_table = rotary_tables(length, HEAD_DIM)
    queries = rotate(qkv[:, 0], cos_table, sin_table).astype(jnp.bfloat16)
    key_rows = rotate(qkv[:, 1], cos_table, sin_table).astype(jnp.bfloat16)
    values = qkv[:, 2].astype(jnp.bfloat16)
    attn_probs = attention_probs(queries, key_rows).astype(jnp.bfloat16)
    mixed = jnp.einsum("hqk,khd->qhd", attn_probs, values, preferred_element_type=jnp.float32)
    mixed = mixed.reshape(length, -1).astype(jnp.bfloat16)
    attn_branch = scatter_rows(mixed, w_out, row_count)
    hidden = layer_input + norm_rows(attn_branch, gains[1])
    mlp_in = norm_rows(hidden, gains[2]).astype(jnp.bfloat16)
    gathered_c, up_act = gather_rows(mlp_in, w_up)
    gelu_out = jax.nn.gelu(up_act, approximate=True).astype(jnp.bfloat16)
    down_branch = scatter_rows(gelu_out, w_down, row_count)
    result = hidden + norm_rows(down_branch, gains[3])
    kept_values = (
        gathered_a,
        queries,
        key_rows,
        values,
        mixed,
        attn_branch,
        hidden,
        gathered_c,
        up_act,
        gelu_out,
        down_branch,
    )
    return (result, kept_values)


def layer_backward(layer_input, grad_result, kept_values, weights):
    gains, w_qkv, w_out, w_up, w_down = weights
    (
        gathered_a,
        queries,
        key_rows,
        values,
        mixed,
        attn_branch,
        hidden,
        gathered_c,
        up_act,
        gelu_out,
        down_branch,
    ) = kept_values
    row_count, model_width = layer_input.shape
    pullback = jax.vjp(norm_rows, down_branch, gains[3])[1]
    grad_down, gain_three = pullback(grad_result)
    gathered_dd, grad_gelu = gather_grads(grad_down.astype(jnp.bfloat16), w_down)
    down_total = contract(gelu_out, gathered_dd)
    pullback = jax.vjp(lambda vector: jax.nn.gelu(vector, approximate=True), up_act)[1]
    grad_up = pullback(grad_gelu)[0].astype(jnp.bfloat16)
    up_total = contract(gathered_c, grad_up)
    grad_mlp = scatter_grads(grad_up, w_up, row_count)
    pullback = jax.vjp(norm_rows, hidden, gains[2])[1]
    grad_norm_mlp, gain_two = pullback(grad_mlp)
    grad_hidden = grad_result + grad_norm_mlp
    pullback = jax.vjp(norm_rows, attn_branch, gains[1])[1]
    grad_attn, gain_one = pullback(grad_hidden)
    gathered_da, grad_mixed = gather_grads(grad_attn.astype(jnp.bfloat16), w_out)
    out_total = contract(mixed, gathered_da)
    length = grad_mixed.shape[0]
    head_count = w_qkv.shape[2] // HEAD_DIM
    grad_mixed = grad_mixed.astype(jnp.bfloat16).reshape(length, head_count, HEAD_DIM)
    attn_probs = attention_probs(queries, key_rows)
    probs_low = attn_probs.astype(jnp.bfloat16)
    grad_probs = jnp.einsum("qhd,khd->hqk", grad_mixed, values, preferred_element_type=jnp.float32)
    grad_values = jnp.einsum(
        "hqk,qhd->khd", probs_low, grad_mixed, preferred_element_type=jnp.float32
    )
    row_dots = jnp.sum(grad_probs * attn_probs, axis=-1, keepdims=True)
    grad_scores = (attn_probs * (grad_probs - row_dots)).astype(jnp.bfloat16)
    scale_value = HEAD_DIM ** (-0.5)
    grad_queries = (
        jnp.einsum("hqk,khd->qhd", grad_scores, key_rows, preferred_element_type=jnp.float32)
        * scale_value
    )
    grad_keys = (
        jnp.einsum("hqk,qhd->khd", grad_scores, queries, preferred_element_type=jnp.float32)
        * scale_value
    )
    cos_table, sin_table = rotary_tables(length, HEAD_DIM)
    pullback = jax.vjp(lambda vector: rotate(vector, cos_table, sin_table), grad_queries)[1]
    grad_q_raw = pullback(grad_queries)[0]
    grad_k_raw = pullback(grad_keys)[0]
    grad_qkv = (
        jnp.stack([grad_q_raw, grad_k_raw, grad_values], axis=1)
        .reshape(length, -1)
        .astype(jnp.bfloat16)
    )
    qkv_total = contract(gathered_a, grad_qkv).reshape(model_width, 3, -1)
    grad_attn_in = scatter_grads(grad_qkv, w_qkv.reshape(model_width, -1), row_count)
    pullback = jax.vjp(norm_rows, layer_input, gains[0])[1]
    grad_norm_in, gain_zero = pullback(grad_attn_in)
    grad_input = grad_hidden + grad_norm_in
    gain_total = jnp.stack([gain_zero, gain_one, gain_two, gain_three])
    return (grad_input, (gain_total, qkv_total, out_total, up_total, down_total))


def lagged(first_section, stacked):
    blank = jnp.zeros_like(stacked[:1])
    earlier = jnp.concatenate([blank, stacked[:-1]])
    later = jnp.concatenate([stacked[1:], blank])
    return jnp.where(first_section, earlier, later)


def per_device(
    inputs,
    out_cotangent,
    group_ids,
    group_weights,
    gains,
    qkv_weight,
    out_weight,
    up_weight,
    down_weight,
):
    weights = (gains[0], qkv_weight[0], out_weight[0], up_weight[0], down_weight[0])
    micro_count, row_count, model_width = inputs.shape
    first_section = lax.axis_index("section") == 0
    group_count = group_weights.shape[0]
    matches = group_ids[..., None] == jnp.arange(group_count, dtype=jnp.int32)
    row_scale = jnp.sum(jnp.where(matches, group_weights, 0.0), axis=-1)
    scaled = out_cotangent.astype(jnp.float32) * row_scale[..., None]
    padded = jnp.concatenate([inputs, jnp.zeros((1, row_count, model_width), jnp.bfloat16)])

    def forward_tick(received, fresh_input):
        layer_input = jnp.where(first_section, fresh_input, received)
        result, kept_values = layer_forward(layer_input.astype(jnp.float32), weights)
        result_low = result.astype(jnp.bfloat16)
        outgoing = shifted(result_low, "section", 1)
        stashed = ()
        return (outgoing, (layer_input, result_low, stashed))

    start_rows = jnp.zeros((row_count, model_width), jnp.bfloat16)
    _, (layer_inputs, layer_results, stashed) = lax.scan(forward_tick, start_rows, padded)
    layer_outputs = jnp.where(first_section, layer_results[:-1], layer_results[1:])[None]
    back_inputs = lagged(first_section, layer_inputs)
    back_stash = jax.tree.map(lambda stacked: lagged(first_section, stacked), stashed)
    grad_padded = jnp.concatenate([scaled, jnp.zeros((1, row_count, model_width), jnp.float32)])
    tick_index = jnp.arange(micro_count + 1, dtype=jnp.int32)
    tick_valid = jnp.where(first_section, tick_index >= 1, tick_index < micro_count).astype(
        jnp.float32
    )

    def backward_tick(carry, step_item):
        received, totals = carry
        layer_input, cotangent, valid_now, stash_now = step_item
        grad_now = jnp.where(first_section, received.astype(jnp.float32), cotangent)
        input_now = layer_input.astype(jnp.float32)
        kept_values = layer_forward(input_now, weights)[1]
        grad_input, layer_grads = layer_backward(input_now, grad_now, kept_values, weights)
        totals = jax.tree.map(lambda total, update: total + valid_now * update, totals, layer_grads)
        grad_low = grad_input.astype(jnp.bfloat16)
        outgoing = shifted(grad_low, "section", -1)
        return ((outgoing, totals), grad_low)

    start_totals = (
        jnp.zeros((4, model_width), jnp.float32),
        jnp.zeros(qkv_weight.shape[1:], jnp.float32),
        jnp.zeros(out_weight.shape[1:], jnp.float32),
        jnp.zeros(up_weight.shape[1:], jnp.float32),
        jnp.zeros(down_weight.shape[1:], jnp.float32),
    )
    (_, totals), grad_lows = lax.scan(
        backward_tick,
        (start_rows, start_totals),
        (back_inputs, grad_padded, tick_valid, back_stash),
    )
    input_grads = jnp.where(first_section, grad_lows[1:], grad_lows[:-1])[None]
    gain_total, qkv_total, out_total, up_total, down_total = totals
    gains_grad = lax.psum_scatter(gain_total, ("dp", "tensor"), scatter_dimension=1, tiled=True)
    qkv_grad, out_grad, up_grad, down_grad = (
        lax.psum_scatter(
            qkv_total.astype(jnp.bfloat16), "dp", scatter_dimension=0, tiled=True
        ).astype(jnp.float32),
        lax.psum_scatter(
            out_total.astype(jnp.bfloat16), "dp", scatter_dimension=1, tiled=True
        ).astype(jnp.float32),
        lax.psum_scatter(
            up_total.astype(jnp.bfloat16), "dp", scatter_dimension=0, tiled=True
        ).astype(jnp.float32),
        lax.psum_scatter(
            down_total.astype(jnp.bfloat16), "dp", scatter_dimension=1, tiled=True
        ).astype(jnp.float32),
    )
    return (
        layer_outputs,
        input_grads,
        gains_grad[None],
        qkv_grad[None],
        out_grad[None],
        up_grad[None],
        down_grad[None],
    )


def solution(mesh):
    placed = (
        P("dp", "tensor", None),
        P("dp", "tensor", None),
        P("dp", "tensor"),
        P(),
        P("section", None, None),
        P("section", None, None, "tensor"),
        P("section", "tensor", None),
        P("section", None, "tensor"),
        P("section", "tensor", None),
    )
    return jax.shard_map(
        per_device,
        mesh=mesh,
        in_specs=placed,
        out_specs=(
            P("section", "dp", "tensor", None),
            P("section", "dp", "tensor", None),
            P("section", None, ("dp", "tensor")),
            P("section", "dp", None, "tensor"),
            P("section", "tensor", "dp"),
            P("section", "dp", "tensor"),
            P("section", "tensor", "dp"),
        ),
        check_vma=False,
    )
```

profile of v0, /device:TPU:0, one launch (start us, length us, event | category | flops | bytes accessed | tf_op | source)
XLA Modules:
  0.0 2998.0 jit_solution(8786126189976020737)
XLA Ops:
  16.6 925.6 %while.41 = (s32[]{:T(128)}, bf16[256,1024]{1,0:T(8,128)(2,1)S(1)}, bf16[3,256,1024]{2,1,0:T(8,128)(2,1)}, bf16[3,256,1024]{2,1,0:T(8,128)(2,1)}, pred[]{:T(512)...) while((s32[]{:T(128)}, bf16[256,1024]{1,0:T(8,128)(2,1)S(1)}, ...), condition=%wide.region_9.10_spmd, body=%wide.region_0.9_spmd.sunk | while | flops 7564986880 | bytes 155824272 | solution.py:247
  20.9 47.9 %all-gather.7.cloned.1.call-done = bf16[1024,1024]{1,0:T(8,128)(2,1)} async-done(((bf16[256,1024]{1,0:T(8,128)(2,1)}), bf16[1024,1024]{1,0:T(8,128)(2,1)}) %all-gather.7.cloned.1.call-update) | async-done | bytes 2097168 | tf_op jit(solution)/shard_map/while/body/eval_jaxpr/all_gather | solution.py:55
  95.7 75.6 %reduce-scatter.24.cloned.1.call-done = f32[256,1024]{1,0:T(8,128)} async-done(((f32[1024,1024]{1,0:T(8,128)}), f32[256,1024]{1,0:T(8,128)}) %reduce-scatter.24.cloned.1.call-update) | async-done | bytes 1048592 | tf_op jit(solution)/shard_map/while/body/eval_jaxpr/reduce_scatter | solution.py:63
  231.9 75.6 %reduce-scatter.26.cloned.1.call-done = f32[256,1024]{1,0:T(8,128)} async-done(((f32[1024,1024]{1,0:T(8,128)}), f32[256,1024]{1,0:T(8,128)}) %reduce-scatter.26.cloned.1.call-update) | async-done | bytes 1048592 | tf_op jit(solution)/shard_map/while/body/eval_jaxpr/reduce_scatter | solution.py:63
  330.2 46.7 %all-gather.7.cloned.1.call-done = bf16[1024,1024]{1,0:T(8,128)(2,1)} async-done(((bf16[256,1024]{1,0:T(8,128)(2,1)}), bf16[1024,1024]{1,0:T(8,128)(2,1)}) %all-gather.7.cloned.1.call-update) | async-done | bytes 2097168 | tf_op jit(solution)/shard_map/while/body/eval_jaxpr/all_gather | solution.py:55
  403.8 75.6 %reduce-scatter.24.cloned.1.call-done = f32[256,1024]{1,0:T(8,128)} async-done(((f32[1024,1024]{1,0:T(8,128)}), f32[256,1024]{1,0:T(8,128)}) %reduce-scatter.24.cloned.1.call-update) | async-done | bytes 1048592 | tf_op jit(solution)/shard_map/while/body/eval_jaxpr/reduce_scatter | solution.py:63
  540.1 75.6 %reduce-scatter.26.cloned.1.call-done = f32[256,1024]{1,0:T(8,128)} async-done(((f32[1024,1024]{1,0:T(8,128)}), f32[256,1024]{1,0:T(8,128)}) %reduce-scatter.26.cloned.1.call-update) | async-done | bytes 1048592 | tf_op jit(solution)/shard_map/while/body/eval_jaxpr/reduce_scatter | solution.py:63
  638.4 46.7 %all-gather.7.cloned.1.call-done = bf16[1024,1024]{1,0:T(8,128)(2,1)} async-done(((bf16[256,1024]{1,0:T(8,128)(2,1)}), bf16[1024,1024]{1,0:T(8,128)(2,1)}) %all-gather.7.cloned.1.call-update) | async-done | bytes 2097168 | tf_op jit(solution)/shard_map/while/body/eval_jaxpr/all_gather | solution.py:55
  712.0 75.6 %reduce-scatter.24.cloned.1.call-done = f32[256,1024]{1,0:T(8,128)} async-done(((f32[1024,1024]{1,0:T(8,128)}), f32[256,1024]{1,0:T(8,128)}) %reduce-scatter.24.cloned.1.call-update) | async-done | bytes 1048592 | tf_op jit(solution)/shard_map/while/body/eval_jaxpr/reduce_scatter | solution.py:63
  848.3 75.6 %reduce-scatter.26.cloned.1.call-done = f32[256,1024]{1,0:T(8,128)} async-done(((f32[1024,1024]{1,0:T(8,128)}), f32[256,1024]{1,0:T(8,128)}) %reduce-scatter.26.cloned.1.call-update) | async-done | bytes 1048592 | tf_op jit(solution)/shard_map/while/body/eval_jaxpr/reduce_scatter | solution.py:63
  948.0 1857.8 %while.42 = (s32[]{:T(128)}, bf16[256,1024]{1,0:T(8,128)(2,1)S(1)}, f32[4,1024]{1,0:T(4,128)S(1)}, f32[1024,3,256]{2,0,1:T(8,128)}, f32[256,1024]{1,0:T(8,128)},...) while((s32[]{:T(128)}, bf16[256,1024]{1,0:T(8,128)(2,1)S(1)}, ...), condition=%wide.region_31.32_spmd.clone, body=%wide.region_11.31_spmd.clone.sunk | while | flops 22695434240 | bytes 623419904 | solution.py:276
  950.4 48.2 %all-gather.11.cloned.1.call-done = bf16[1024,1024]{1,0:T(8,128)(2,1)} async-done(((bf16[256,1024]{1,0:T(8,128)(2,1)}), bf16[1024,1024]{1,0:T(8,128)(2,1)}) %all-gather.11.cloned.1.call-update) | async-done | bytes 2097168 | tf_op jit(solution)/shard_map/while/body/eval_jaxpr/all_gather | solution.py:55
  1027.8 75.6 %reduce-scatter.28.cloned.1.call-done = f32[256,1024]{1,0:T(8,128)} async-done(((f32[1024,1024]{1,0:T(8,128)}), f32[256,1024]{1,0:T(8,128)}) %reduce-scatter.28.cloned.1.call-update) | async-done | bytes 1048592 | tf_op jit(solution)/shard_map/while/body/eval_jaxpr/reduce_scatter | solution.py:63
  1165.3 75.6 %reduce-scatter.30.cloned.1.call-done = f32[256,1024]{1,0:T(8,128)} async-done(((f32[1024,1024]{1,0:T(8,128)}), f32[256,1024]{1,0:T(8,128)}) %reduce-scatter.30.cloned.1.call-update) | async-done | bytes 1048592 | tf_op jit(solution)/shard_map/while/body/eval_jaxpr/reduce_scatter | solution.py:63
  1306.9 75.6 %reduce-scatter.32.cloned.1.call-done = f32[256,1024]{1,0:T(8,128)} async-done(((f32[1024,1024]{1,0:T(8,128)}), f32[256,1024]{1,0:T(8,128)}) %reduce-scatter.32.cloned.1.call-update) | async-done | bytes 1048592 | tf_op jit(solution)/shard_map/while/body/eval_jaxpr/reduce_scatter | solution.py:84
  1491.5 56.0 %reduce-scatter.34.cloned.1.call-done = f32[256,1024]{1,0:T(8,128)} async-done(((f32[1024,1024]{1,0:T(8,128)}), f32[256,1024]{1,0:T(8,128)}) %reduce-scatter.34.cloned.1.call-update) | async-done | bytes 1048592 | tf_op jit(solution)/shard_map/while/body/eval_jaxpr/reduce_scatter | solution.py:84
  1645.8 75.6 %reduce-scatter.28.cloned.1.call-done = f32[256,1024]{1,0:T(8,128)} async-done(((f32[1024,1024]{1,0:T(8,128)}), f32[256,1024]{1,0:T(8,128)}) %reduce-scatter.28.cloned.1.call-update) | async-done | bytes 1048592 | tf_op jit(solution)/shard_map/while/body/eval_jaxpr/reduce_scatter | solution.py:63
  1783.3 75.6 %reduce-scatter.30.cloned.1.call-done = f32[256,1024]{1,0:T(8,128)} async-done(((f32[1024,1024]{1,0:T(8,128)}), f32[256,1024]{1,0:T(8,128)}) %reduce-scatter.30.cloned.1.call-update) | async-done | bytes 1048592 | tf_op jit(solution)/shard_map/while/body/eval_jaxpr/reduce_scatter | solution.py:63
  1924.9 75.6 %reduce-scatter.32.cloned.1.call-done = f32[256,1024]{1,0:T(8,128)} async-done(((f32[1024,1024]{1,0:T(8,128)}), f32[256,1024]{1,0:T(8,128)}) %reduce-scatter.32.cloned.1.call-update) | async-done | bytes 1048592 | tf_op jit(solution)/shard_map/while/body/eval_jaxpr/reduce_scatter | solution.py:84
  2113.3 52.2 %reduce-scatter.34.cloned.1.call-done = f32[256,1024]{1,0:T(8,128)} async-done(((f32[1024,1024]{1,0:T(8,128)}), f32[256,1024]{1,0:T(8,128)}) %reduce-scatter.34.cloned.1.call-update) | async-done | bytes 1048592 | tf_op jit(solution)/shard_map/while/body/eval_jaxpr/reduce_scatter | solution.py:84
  2263.8 75.6 %reduce-scatter.28.cloned.1.call-done = f32[256,1024]{1,0:T(8,128)} async-done(((f32[1024,1024]{1,0:T(8,128)}), f32[256,1024]{1,0:T(8,128)}) %reduce-scatter.28.cloned.1.call-update) | async-done | bytes 1048592 | tf_op jit(solution)/shard_map/while/body/eval_jaxpr/reduce_scatter | solution.py:63
  2401.3 75.6 %reduce-scatter.30.cloned.1.call-done = f32[256,1024]{1,0:T(8,128)} async-done(((f32[1024,1024]{1,0:T(8,128)}), f32[256,1024]{1,0:T(8,128)}) %reduce-scatter.30.cloned.1.call-update) | async-done | bytes 1048592 | tf_op jit(solution)/shard_map/while/body/eval_jaxpr/reduce_scatter | solution.py:63
  2542.8 75.6 %reduce-scatter.32.cloned.1.call-done = f32[256,1024]{1,0:T(8,128)} async-done(((f32[1024,1024]{1,0:T(8,128)}), f32[256,1024]{1,0:T(8,128)}) %reduce-scatter.32.cloned.1.call-update) | async-done | bytes 1048592 | tf_op jit(solution)/shard_map/while/body/eval_jaxpr/reduce_scatter | solution.py:84
  2731.0 52.4 %reduce-scatter.34.cloned.1.call-done = f32[256,1024]{1,0:T(8,128)} async-done(((f32[1024,1024]{1,0:T(8,128)}), f32[256,1024]{1,0:T(8,128)}) %reduce-scatter.34.cloned.1.call-update) | async-done | bytes 1048592 | tf_op jit(solution)/shard_map/while/body/eval_jaxpr/reduce_scatter | solution.py:84
  (575 shorter events, 1493.3 us)
Async XLA Ops:
  19.9 151.3 %reduce-scatter.24.cloned.1.call-start = ((), (), s32[]{:S(2)}) async-start(), calls=%async_computation.17 | async-start | bytes 5242880 | tf_op jit(solution)/shard_map/while/body/eval_jaxpr/reduce_scatter | solution.py:63
  176.6 131.0 %reduce-scatter.26.cloned.1.call-start = ((), (), s32[]{:S(2)}) async-start(), calls=%async_computation.19 | async-start | bytes 5242880 | tf_op jit(solution)/shard_map/while/body/eval_jaxpr/reduce_scatter | solution.py:63
  329.2 150.2 %reduce-scatter.24.cloned.1.call-start = ((), (), s32[]{:S(2)}) async-start(), calls=%async_computation.17 | async-start | bytes 5242880 | tf_op jit(solution)/shard_map/while/body/eval_jaxpr/reduce_scatter | solution.py:63
  484.7 131.0 %reduce-scatter.26.cloned.1.call-start = ((), (), s32[]{:S(2)}) async-start(), calls=%async_computation.19 | async-start | bytes 5242880 | tf_op jit(solution)/shard_map/while/body/eval_jaxpr/reduce_scatter | solution.py:63
  637.5 150.2 %reduce-scatter.24.cloned.1.call-start = ((), (), s32[]{:S(2)}) async-start(), calls=%async_computation.17 | async-start | bytes 5242880 | tf_op jit(solution)/shard_map/while/body/eval_jaxpr/reduce_scatter | solution.py:63
  712.0 127.6 %all-gather.9.cloned.1.call-start = ((), (), s32[]{:S(2)}) async-start(), calls=%async_computation.18 | async-start | bytes 2621440 | tf_op jit(solution)/shard_map/while/body/eval_jaxpr/all_gather | solution.py:55
  793.0 131.0 %reduce-scatter.26.cloned.1.call-start = ((), (), s32[]{:S(2)}) async-start(), calls=%async_computation.19 | async-start | bytes 5242880 | tf_op jit(solution)/shard_map/while/body/eval_jaxpr/reduce_scatter | solution.py:63
  949.5 153.9 %reduce-scatter.28.cloned.1.call-start = ((), (), s32[]{:S(2)}) async-start(), calls=%async_computation.21 | async-start | bytes 5242880 | tf_op jit(solution)/shard_map/while/body/eval_jaxpr/reduce_scatter | solution.py:63
  1107.4 133.5 %reduce-scatter.30.cloned.1.call-start = ((), (), s32[]{:S(2)}) async-start(), calls=%async_computation.23 | async-start | bytes 5242880 | tf_op jit(solution)/shard_map/while/body/eval_jaxpr/reduce_scatter | solution.py:63
  1165.2 128.0 %all-gather.15.cloned.1.call-start = ((), (), s32[]{:S(2)}) async-start(), calls=%async_computation.24 | async-start | bytes 2621440 | tf_op jit(solution)/shard_map/while/body/eval_jaxpr/all_gather | solution.py:76
  1246.6 135.8 %reduce-scatter.32.cloned.1.call-start = ((), (), s32[]{:S(2)}) async-start(), calls=%async_computation.25 | async-start | bytes 5242880 | tf_op jit(solution)/shard_map/while/body/eval_jaxpr/reduce_scatter | solution.py:84
  1387.3 160.2 %reduce-scatter.34.cloned.1.call-start = ((), (), s32[]{:S(2)}) async-start(), calls=%async_computation.27 | async-start | bytes 5242880 | tf_op jit(solution)/shard_map/while/body/eval_jaxpr/reduce_scatter | solution.py:84
  1569.4 152.0 %reduce-scatter.28.cloned.1.call-start = ((), (), s32[]{:S(2)}) async-start(), calls=%async_computation.21 | async-start | bytes 5242880 | tf_op jit(solution)/shard_map/while/body/eval_jaxpr/reduce_scatter | solution.py:63
  1725.4 133.5 %reduce-scatter.30.cloned.1.call-start = ((), (), s32[]{:S(2)}) async-start(), calls=%async_computation.23 | async-start | bytes 5242880 | tf_op jit(solution)/shard_map/while/body/eval_jaxpr/reduce_scatter | solution.py:63
  1783.3 128.0 %all-gather.15.cloned.1.call-start = ((), (), s32[]{:S(2)}) async-start(), calls=%async_computation.24 | async-start | bytes 2621440 | tf_op jit(solution)/shard_map/while/body/eval_jaxpr/all_gather | solution.py:76
  1864.6 135.8 %reduce-scatter.32.cloned.1.call-start = ((), (), s32[]{:S(2)}) async-start(), calls=%async_computation.25 | async-start | bytes 5242880 | tf_op jit(solution)/shard_map/while/body/eval_jaxpr/reduce_scatter | solution.py:84
  2005.4 160.2 %reduce-scatter.34.cloned.1.call-start = ((), (), s32[]{:S(2)}) async-start(), calls=%async_computation.27 | async-start | bytes 5242880 | tf_op jit(solution)/shard_map/while/body/eval_jaxpr/reduce_scatter | solution.py:84
  2187.3 152.0 %reduce-scatter.28.cloned.1.call-start = ((), (), s32[]{:S(2)}) async-start(), calls=%async_computation.21 | async-start | bytes 5242880 | tf_op jit(solution)/shard_map/while/body/eval_jaxpr/reduce_scatter | solution.py:63
  2343.3 133.5 %reduce-scatter.30.cloned.1.call-start = ((), (), s32[]{:S(2)}) async-start(), calls=%async_computation.23 | async-start | bytes 5242880 | tf_op jit(solution)/shard_map/while/body/eval_jaxpr/reduce_scatter | solution.py:63
  2401.2 128.0 %all-gather.15.cloned.1.call-start = ((), (), s32[]{:S(2)}) async-start(), calls=%async_computation.24 | async-start | bytes 2621440 | tf_op jit(solution)/shard_map/while/body/eval_jaxpr/all_gather | solution.py:76
  2482.6 135.8 %reduce-scatter.32.cloned.1.call-start = ((), (), s32[]{:S(2)}) async-start(), calls=%async_computation.25 | async-start | bytes 5242880 | tf_op jit(solution)/shard_map/while/body/eval_jaxpr/reduce_scatter | solution.py:84
  2623.3 160.2 %reduce-scatter.34.cloned.1.call-start = ((), (), s32[]{:S(2)}) async-start(), calls=%async_computation.27 | async-start | bytes 5242880 | tf_op jit(solution)/shard_map/while/body/eval_jaxpr/reduce_scatter | solution.py:84
  2812.4 141.8 %reduce-scatter.20.cloned.1.call-start = ((), (), s32[]{:S(2)}) async-start(), calls=%async_computation.14 | async-start | bytes 2621440 | tf_op jit(solution)/shard_map/reduce_scatter | solution.py:294
  2816.3 171.8 %reduce-scatter.18.cloned.1.call-start = ((), (), s32[]{:S(2)}) async-start(), calls=%async_computation.13 | async-start | bytes 2621440 | tf_op jit(solution)/shard_map/reduce_scatter | solution.py:291
  (127 other events, 4695.7 us)
Sparse Core Ops, SparseCore 0:
  20.0 48.6 all-gather.6
  95.7 75.4 reduce-scatter.23
  232.1 75.4 reduce-scatter.25
  329.4 47.4 all-gather.6
  403.9 75.4 reduce-scatter.23
  540.2 75.4 reduce-scatter.25
  637.6 47.4 all-gather.6
  712.1 75.4 reduce-scatter.23
  848.4 75.4 reduce-scatter.25
  951.1 47.4 all-gather.10
  1027.9 75.4 reduce-scatter.27
  1165.4 75.4 reduce-scatter.29
  1306.9 75.4 reduce-scatter.31
  1387.4 46.4 all-gather.16
  1472.0 75.4 reduce-scatter.33
  1645.9 75.4 reduce-scatter.27
  1783.4 75.4 reduce-scatter.29
  1925.0 75.4 reduce-scatter.31
  2005.5 46.4 all-gather.16
  2090.0 75.4 reduce-scatter.33
  2263.8 75.4 reduce-scatter.27
  2401.3 75.4 reduce-scatter.29
  2542.9 75.4 reduce-scatter.31
  2707.9 75.4 reduce-scatter.33
  (12 shorter events, 555.0 us)
Sparse Core Ops, SparseCore 1:
  2810.4 55.4 reduce-scatter.21
  2868.9 20.5 reduce-scatter.15
  2892.0 28.1 reduce-scatter.13
  2922.8 31.3 reduce-scatter.19
  2956.7 31.3 reduce-scatter.17
where the time goes:
time: 3010 us; the launch traced here: 3000 us
  waiting for transfers between devices  2350 us (78%)
  matrix products  391 us (13%)
  other arithmetic  161 us (5%)
  local copies, waits for them, and re-layouts  45.5 us (2%)
    reduce_scatter x12, waiting for transfers between devices, scatter_rows(): lax.psum_scatter(partial_term(jnp.int32(0), lax.axis_size('tensor') * row...  907 us
    all_gather x12, waiting for transfers between devices, gather_rows(): lax.all_gather(row_values, 'tensor', axis=0, tiled=True)  549 us
    reduce_scatter x6, waiting for transfers between devices, scatter_grads(): lax.psum_scatter(partial_term(jnp.int32(0), lax.axis_size('tensor') * row...  387 us
    all_gather x6, waiting for transfers between devices, gather_grads(): lax.all_gather(row_values, 'tensor', axis=0, tiled=True)  279 us
    ppermute x6, waiting for transfers between devices, shifted(): return lax.ppermute(block, axis, route)  69.5 us
    dot_general x12, matrix products, contract(): lax.dot_general(left_rows, right_rows, (((0,), (0,)), ((), ())), preferre...  63 us
    sub x6, matrix products, attention_probs(): expos = jnp.exp(scores - jnp.max(scores, axis=-1, keepdims=True))  62.7 us
    dot_general x12, matrix products, partial_term(): return jnp.dot(row_values, weight, preferred_element_type=jnp.float32)  62.4 us
  transfers between devices with their start and end apart: 47, of which 47 were waited for; matrix products, arithmetic and copies ran while one was open for 3% of the time, Pallas kernels for 0%

commit v1 on v0

--- a/solution.py
+++ b/solution.py
@@ -5,6 +5,27 @@
 
 HEAD_DIM = 64
 NORM_EPSILON = 1e-06
+
+
+def gather_around(x, axis, dim):
+    size, index, extent = (lax.axis_size(axis), lax.axis_index(axis), x.shape[dim])
+    right = [(i, (i + 1) % size) for i in range(size)]
+    left = [(i, (i - 1) % size) for i in range(size)]
+    result = jnp.zeros((*x.shape[:dim], size * extent, *x.shape[dim + 1 :]), x.dtype)
+    result = lax.dynamic_update_slice_in_dim(result, x, index * extent, axis=dim)
+    from_left = from_right = x
+    half = size // 2
+    for step in range(1, half + 1):
+        from_left = lax.ppermute(from_left, axis, right)
+        result = lax.dynamic_update_slice_in_dim(
+            result, from_left, (index - step) % size * extent, axis=dim
+        )
+        if step < size - half:
+            from_right = lax.ppermute(from_right, axis, left)
+            result = lax.dynamic_update_slice_in_dim(
+                result, from_right, (index + step) % size * extent, axis=dim
+            )
+    return result
 
 
 def shifted(block, axis, distance):
@@ -52,7 +73,7 @@
     def project(shard_rows, offset):
         return (shard_rows, jnp.dot(shard_rows, weight, preferred_element_type=jnp.float32))
 
-    return project(lax.all_gather(row_values, "tensor", axis=0, tiled=True), jnp.int32(0))
+    return project(gather_around(row_values, "tensor", 0), jnp.int32(0))
 
 
 def scatter_rows(row_values, weight, row_count):

time: 3010 us -> 2920 us (0.970)
  waiting for transfers between devices: 2350 us -> 2060 us
  starting transfers between devices: 28.6 us -> 153 us
  local copies, waits for them, and re-layouts: 45.5 us -> 124 us
    all_gather x12 -> x0, waiting for transfers between devices: 549 us -> none  [gather_rows(): lax.all_gather(row_values, 'tensor', axis=0, tiled=True)]
    ppermute x0 -> x36, waiting for transfers between devices: none -> 256 us  [the longest x24 237 us: gather_around(): from_left = lax.ppermute(from_left, axis, right)]
    ppermute x0 -> x36, starting transfers between devices: none -> 138 us  [the longest x24 110 us: gather_around(): from_left = lax.ppermute(from_left, axis, right)]
    dynamic_update_slice x0 -> x42, local copies, waits for them, and re-layouts: none -> 38 us  [the longest x24 21.9 us: gather_around(): lax.dynamic_update_slice_in_dim(result, from_left, (index - step) % size...]
  transfers between devices with their start and end apart: 47 -> 71, of which waited for: 47 -> 68; matrix products, arithmetic and copies ran while one was open for 3% -> 5% of each run, Pallas kernels for 0% -> 0%
where the time goes in v1:
time: 2920 us; the launch traced here: 2900 us
  waiting for transfers between devices  2060 us (71%)
  matrix products  389 us (13%)
  other arithmetic  154 us (5%)
  starting transfers between devices  153 us (5%)
  local copies, waits for them, and re-layouts  124 us (4%)
    reduce_scatter x12, waiting for transfers between devices, scatter_rows(): lax.psum_scatter(partial_term(jnp.int32(0), lax.axis_size('tensor') * row...  911 us
    reduce_scatter x6, waiting for transfers between devices, scatter_grads(): lax.psum_scatter(partial_term(jnp.int32(0), lax.axis_size('tensor') * row...  386 us
    all_gather x6, waiting for transfers between devices, gather_grads(): lax.all_gather(row_values, 'tensor', axis=0, tiled=True)  279 us
    ppermute x24, waiting for transfers between devices, gather_around(): from_left = lax.ppermute(from_left, axis, right)  237 us
    ppermute x24, starting transfers between devices, gather_around(): from_left = lax.ppermute(from_left, axis, right)  110 us
    ppermute x6, waiting for transfers between devices, shifted(): return lax.ppermute(block, axis, route)  69.4 us
    dot_general x12, matrix products, partial_term(): return jnp.dot(row_values, weight, preferred_element_type=jnp.float32)  64.6 us
    dot_general x12, matrix products, contract(): lax.dot_general(left_rows, right_rows, (((0,), (0,)), ((), ())), preferre...  64.2 us
  transfers between devices with their start and end apart: 71, of which 68 were waited for; matrix products, arithmetic and copies ran while one was open for 5% of the time, Pallas kernels for 0%

profile of v1, /device:TPU:0, one launch (start us, length us, event | category | flops | bytes accessed | tf_op | source)
XLA Modules:
  0.0 2903.3 jit_solution(3991799308101972285)
XLA Ops:
  15.4 876.5 %while.41 = (s32[]{:T(128)}, bf16[256,1024]{1,0:T(8,128)(2,1)S(1)}, bf16[3,256,1024]{2,1,0:T(8,128)(2,1)}, bf16[3,256,1024]{2,1,0:T(8,128)(2,1)}, pred[]{:T(512)...) while((s32[]{:T(128)}, bf16[256,1024]{1,0:T(8,128)(2,1)S(1)}, ...), condition=%wide.region_9.10_spmd, body=%wide.region_0.9_spmd.sunk | while | flops 7564986880 | bytes 166310864 | solution.py:268
  84.2 76.2 %reduce-scatter.24.cloned.1.call-done = f32[256,1024]{1,0:T(8,128)} async-done(((f32[1024,1024]{1,0:T(8,128)}), f32[256,1024]{1,0:T(8,128)}) %reduce-scatter.24.cloned.1.call-update) | async-done | bytes 1048592 | tf_op jit(solution)/shard_map/while/body/eval_jaxpr/reduce_scatter | solution.py:84
  214.5 76.0 %reduce-scatter.26.cloned.1.call-done = f32[256,1024]{1,0:T(8,128)} async-done(((f32[1024,1024]{1,0:T(8,128)}), f32[256,1024]{1,0:T(8,128)}) %reduce-scatter.26.cloned.1.call-update) | async-done | bytes 1048592 | tf_op jit(solution)/shard_map/while/body/eval_jaxpr/reduce_scatter | solution.py:84
  375.3 76.6 %reduce-scatter.24.cloned.1.call-done = f32[256,1024]{1,0:T(8,128)} async-done(((f32[1024,1024]{1,0:T(8,128)}), f32[256,1024]{1,0:T(8,128)}) %reduce-scatter.24.cloned.1.call-update) | async-done | bytes 1048592 | tf_op jit(solution)/shard_map/while/body/eval_jaxpr/reduce_scatter | solution.py:84
  506.0 76.0 %reduce-scatter.26.cloned.1.call-done = f32[256,1024]{1,0:T(8,128)} async-done(((f32[1024,1024]{1,0:T(8,128)}), f32[256,1024]{1,0:T(8,128)}) %reduce-scatter.26.cloned.1.call-update) | async-done | bytes 1048592 | tf_op jit(solution)/shard_map/while/body/eval_jaxpr/reduce_scatter | solution.py:84
  666.8 76.6 %reduce-scatter.24.cloned.1.call-done = f32[256,1024]{1,0:T(8,128)} async-done(((f32[1024,1024]{1,0:T(8,128)}), f32[256,1024]{1,0:T(8,128)}) %reduce-scatter.24.cloned.1.call-update) | async-done | bytes 1048592 | tf_op jit(solution)/shard_map/while/body/eval_jaxpr/reduce_scatter | solution.py:84
  797.5 76.0 %reduce-scatter.26.cloned.1.call-done = f32[256,1024]{1,0:T(8,128)} async-done(((f32[1024,1024]{1,0:T(8,128)}), f32[256,1024]{1,0:T(8,128)}) %reduce-scatter.26.cloned.1.call-update) | async-done | bytes 1048592 | tf_op jit(solution)/shard_map/while/body/eval_jaxpr/reduce_scatter | solution.py:84
  897.6 1813.5 %while.42 = (s32[]{:T(128)}, bf16[256,1024]{1,0:T(8,128)(2,1)S(1)}, f32[4,1024]{1,0:T(4,128)}, f32[1024,3,256]{2,0,1:T(8,128)}, f32[256,1024]{1,0:T(8,128)}, /*i...) while((s32[]{:T(128)}, bf16[256,1024]{1,0:T(8,128)(2,1)S(1)}, ...), condition=%wide.region_31.32_spmd.clone, body=%wide.region_11.31_spmd.clone.sunk | while | flops 22695434240 | bytes 637363712 | solution.py:297
  967.5 76.5 %reduce-scatter.28.cloned.1.call-done = f32[256,1024]{1,0:T(8,128)} async-done(((f32[1024,1024]{1,0:T(8,128)}), f32[256,1024]{1,0:T(8,128)}) %reduce-scatter.28.cloned.1.call-update) | async-done | bytes 1048592 | tf_op jit(solution)/shard_map/while/body/eval_jaxpr/reduce_scatter | solution.py:84
  1099.1 76.0 %reduce-scatter.30.cloned.1.call-done = f32[256,1024]{1,0:T(8,128)} async-done(((f32[1024,1024]{1,0:T(8,128)}), f32[256,1024]{1,0:T(8,128)}) %reduce-scatter.30.cloned.1.call-update) | async-done | bytes 1048592 | tf_op jit(solution)/shard_map/while/body/eval_jaxpr/reduce_scatter | solution.py:84
  1180.8 46.6 %all-gather.3.cloned.1.call-done = bf16[1024,1024]{1,0:T(8,128)(2,1)} async-done(((bf16[256,1024]{1,0:T(8,128)(2,1)}), bf16[1024,1024]{1,0:T(8,128)(2,1)}) %all-gather.3.cloned.1.call-update) | async-done | bytes 2097168 | tf_op jit(solution)/shard_map/while/body/eval_jaxpr/all_gather | solution.py:97
  1241.1 75.6 %reduce-scatter.32.cloned.1.call-done = f32[256,1024]{1,0:T(8,128)} async-done(((f32[1024,1024]{1,0:T(8,128)}), f32[256,1024]{1,0:T(8,128)}) %reduce-scatter.32.cloned.1.call-update) | async-done | bytes 1048592 | tf_op jit(solution)/shard_map/while/body/eval_jaxpr/reduce_scatter | solution.py:105
  1321.6 46.5 %all-gather.5.cloned.1.call-done = bf16[1024,1024]{1,0:T(8,128)(2,1)} async-done(((bf16[256,1024]{1,0:T(8,128)(2,1)}), bf16[1024,1024]{1,0:T(8,128)(2,1)}) %all-gather.5.cloned.1.call-update) | async-done | bytes 2097168 | tf_op jit(solution)/shard_map/while/body/eval_jaxpr/all_gather | solution.py:97
  1427.3 54.8 %reduce-scatter.34.cloned.1.call-done = f32[256,1024]{1,0:T(8,128)} async-done(((f32[1024,1024]{1,0:T(8,128)}), f32[256,1024]{1,0:T(8,128)}) %reduce-scatter.34.cloned.1.call-update) | async-done | bytes 1048592 | tf_op jit(solution)/shard_map/while/body/eval_jaxpr/reduce_scatter | solution.py:105
  1572.6 74.7 %reduce-scatter.28.cloned.1.call-done = f32[256,1024]{1,0:T(8,128)} async-done(((f32[1024,1024]{1,0:T(8,128)}), f32[256,1024]{1,0:T(8,128)}) %reduce-scatter.28.cloned.1.call-update) | async-done | bytes 1048592 | tf_op jit(solution)/shard_map/while/body/eval_jaxpr/reduce_scatter | solution.py:84
  1702.3 76.0 %reduce-scatter.30.cloned.1.call-done = f32[256,1024]{1,0:T(8,128)} async-done(((f32[1024,1024]{1,0:T(8,128)}), f32[256,1024]{1,0:T(8,128)}) %reduce-scatter.30.cloned.1.call-update) | async-done | bytes 1048592 | tf_op jit(solution)/shard_map/while/body/eval_jaxpr/reduce_scatter | solution.py:84
  1844.3 75.6 %reduce-scatter.32.cloned.1.call-done = f32[256,1024]{1,0:T(8,128)} async-done(((f32[1024,1024]{1,0:T(8,128)}), f32[256,1024]{1,0:T(8,128)}) %reduce-scatter.32.cloned.1.call-update) | async-done | bytes 1048592 | tf_op jit(solution)/shard_map/while/body/eval_jaxpr/reduce_scatter | solution.py:105
  1924.8 46.6 %all-gather.5.cloned.1.call-done = bf16[1024,1024]{1,0:T(8,128)(2,1)} async-done(((bf16[256,1024]{1,0:T(8,128)(2,1)}), bf16[1024,1024]{1,0:T(8,128)(2,1)}) %all-gather.5.cloned.1.call-update) | async-done | bytes 2097168 | tf_op jit(solution)/shard_map/while/body/eval_jaxpr/all_gather | solution.py:97
  2033.4 52.2 %reduce-scatter.34.cloned.1.call-done = f32[256,1024]{1,0:T(8,128)} async-done(((f32[1024,1024]{1,0:T(8,128)}), f32[256,1024]{1,0:T(8,128)}) %reduce-scatter.34.cloned.1.call-update) | async-done | bytes 1048592 | tf_op jit(solution)/shard_map/while/body/eval_jaxpr/reduce_scatter | solution.py:105
  2175.9 74.7 %reduce-scatter.28.cloned.1.call-done = f32[256,1024]{1,0:T(8,128)} async-done(((f32[1024,1024]{1,0:T(8,128)}), f32[256,1024]{1,0:T(8,128)}) %reduce-scatter.28.cloned.1.call-update) | async-done | bytes 1048592 | tf_op jit(solution)/shard_map/while/body/eval_jaxpr/reduce_scatter | solution.py:84
  2305.5 76.0 %reduce-scatter.30.cloned.1.call-done = f32[256,1024]{1,0:T(8,128)} async-done(((f32[1024,1024]{1,0:T(8,128)}), f32[256,1024]{1,0:T(8,128)}) %reduce-scatter.30.cloned.1.call-update) | async-done | bytes 1048592 | tf_op jit(solution)/shard_map/while/body/eval_jaxpr/reduce_scatter | solution.py:84
  2447.6 75.6 %reduce-scatter.32.cloned.1.call-done = f32[256,1024]{1,0:T(8,128)} async-done(((f32[1024,1024]{1,0:T(8,128)}), f32[256,1024]{1,0:T(8,128)}) %reduce-scatter.32.cloned.1.call-update) | async-done | bytes 1048592 | tf_op jit(solution)/shard_map/while/body/eval_jaxpr/reduce_scatter | solution.py:105
  2528.1 46.6 %all-gather.5.cloned.1.call-done = bf16[1024,1024]{1,0:T(8,128)(2,1)} async-done(((bf16[256,1024]{1,0:T(8,128)(2,1)}), bf16[1024,1024]{1,0:T(8,128)(2,1)}) %all-gather.5.cloned.1.call-update) | async-done | bytes 2097168 | tf_op jit(solution)/shard_map/while/body/eval_jaxpr/all_gather | solution.py:97
  2636.4 52.2 %reduce-scatter.34.cloned.1.call-done = f32[256,1024]{1,0:T(8,128)} async-done(((f32[1024,1024]{1,0:T(8,128)}), f32[256,1024]{1,0:T(8,128)}) %reduce-scatter.34.cloned.1.call-update) | async-done | bytes 1048592 | tf_op jit(solution)/shard_map/while/body/eval_jaxpr/reduce_scatter | solution.py:105
  (755 shorter events, 1398.3 us)
Async XLA Ops:
  15.4 145.0 %reduce-scatter.24.cloned.1.call-start = ((), (), s32[]{:S(2)}) async-start(), calls=%async_computation.16 | async-start | bytes 5242880 | tf_op jit(solution)/shard_map/while/body/eval_jaxpr/reduce_scatter | solution.py:84
  84.1 206.4 %reduce-scatter.26.cloned.1.call-start = ((), (), s32[]{:S(2)}) async-start(), calls=%async_computation.17 | async-start | bytes 5242880 | tf_op jit(solution)/shard_map/while/body/eval_jaxpr/reduce_scatter | solution.py:84
  308.8 143.0 %reduce-scatter.24.cloned.1.call-start = ((), (), s32[]{:S(2)}) async-start(), calls=%async_computation.16 | async-start | bytes 5242880 | tf_op jit(solution)/shard_map/while/body/eval_jaxpr/reduce_scatter | solution.py:84
  375.2 206.8 %reduce-scatter.26.cloned.1.call-start = ((), (), s32[]{:S(2)}) async-start(), calls=%async_computation.17 | async-start | bytes 5242880 | tf_op jit(solution)/shard_map/while/body/eval_jaxpr/reduce_scatter | solution.py:84
  600.3 143.1 %reduce-scatter.24.cloned.1.call-start = ((), (), s32[]{:S(2)}) async-start(), calls=%async_computation.16 | async-start | bytes 5242880 | tf_op jit(solution)/shard_map/while/body/eval_jaxpr/reduce_scatter | solution.py:84
  666.7 206.8 %reduce-scatter.26.cloned.1.call-start = ((), (), s32[]{:S(2)}) async-start(), calls=%async_computation.17 | async-start | bytes 5242880 | tf_op jit(solution)/shard_map/while/body/eval_jaxpr/reduce_scatter | solution.py:84
  897.6 146.5 %reduce-scatter.28.cloned.1.call-start = ((), (), s32[]{:S(2)}) async-start(), calls=%async_computation.18 | async-start | bytes 5242880 | tf_op jit(solution)/shard_map/while/body/eval_jaxpr/reduce_scatter | solution.py:84
  967.5 207.5 %reduce-scatter.30.cloned.1.call-start = ((), (), s32[]{:S(2)}) async-start(), calls=%async_computation.19 | async-start | bytes 5242880 | tf_op jit(solution)/shard_map/while/body/eval_jaxpr/reduce_scatter | solution.py:84
  1099.0 128.4 %all-gather.3.cloned.1.call-start = ((), (), s32[]{:S(2)}) async-start(), calls=%async_computation.20 | async-start | bytes 2621440 | tf_op jit(solution)/shard_map/while/body/eval_jaxpr/all_gather | solution.py:97
  1180.8 136.0 %reduce-scatter.32.cloned.1.call-start = ((), (), s32[]{:S(2)}) async-start(), calls=%async_computation.21 | async-start | bytes 5242880 | tf_op jit(solution)/shard_map/while/body/eval_jaxpr/reduce_scatter | solution.py:105
  1321.6 160.6 %reduce-scatter.34.cloned.1.call-start = ((), (), s32[]{:S(2)}) async-start(), calls=%async_computation.23 | async-start | bytes 5242880 | tf_op jit(solution)/shard_map/while/body/eval_jaxpr/reduce_scatter | solution.py:105
  1502.7 144.6 %reduce-scatter.28.cloned.1.call-start = ((), (), s32[]{:S(2)}) async-start(), calls=%async_computation.18 | async-start | bytes 5242880 | tf_op jit(solution)/shard_map/while/body/eval_jaxpr/reduce_scatter | solution.py:84
  1572.6 205.7 %reduce-scatter.30.cloned.1.call-start = ((), (), s32[]{:S(2)}) async-start(), calls=%async_computation.19 | async-start | bytes 5242880 | tf_op jit(solution)/shard_map/while/body/eval_jaxpr/reduce_scatter | solution.py:84
  1702.2 128.4 %all-gather.3.cloned.1.call-start = ((), (), s32[]{:S(2)}) async-start(), calls=%async_computation.20 | async-start | bytes 2621440 | tf_op jit(solution)/shard_map/while/body/eval_jaxpr/all_gather | solution.py:97
  1784.0 135.9 %reduce-scatter.32.cloned.1.call-start = ((), (), s32[]{:S(2)}) async-start(), calls=%async_computation.21 | async-start | bytes 5242880 | tf_op jit(solution)/shard_map/while/body/eval_jaxpr/reduce_scatter | solution.py:105
  1844.3 127.1 %all-gather.5.cloned.1.call-start = ((), (), s32[]{:S(2)}) async-start(), calls=%async_computation.22 | async-start | bytes 2621440 | tf_op jit(solution)/shard_map/while/body/eval_jaxpr/all_gather | solution.py:97
  1924.8 160.8 %reduce-scatter.34.cloned.1.call-start = ((), (), s32[]{:S(2)}) async-start(), calls=%async_computation.23 | async-start | bytes 5242880 | tf_op jit(solution)/shard_map/while/body/eval_jaxpr/reduce_scatter | solution.py:105
  2106.0 144.6 %reduce-scatter.28.cloned.1.call-start = ((), (), s32[]{:S(2)}) async-start(), calls=%async_computation.18 | async-start | bytes 5242880 | tf_op jit(solution)/shard_map/while/body/eval_jaxpr/reduce_scatter | solution.py:84
  2175.8 205.7 %reduce-scatter.30.cloned.1.call-start = ((), (), s32[]{:S(2)}) async-start(), calls=%async_computation.19 | async-start | bytes 5242880 | tf_op jit(solution)/shard_map/while/body/eval_jaxpr/reduce_scatter | solution.py:84
  2305.5 128.4 %all-gather.3.cloned.1.call-start = ((), (), s32[]{:S(2)}) async-start(), calls=%async_computation.20 | async-start | bytes 2621440 | tf_op jit(solution)/shard_map/while/body/eval_jaxpr/all_gather | solution.py:97
  2387.3 135.9 %reduce-scatter.32.cloned.1.call-start = ((), (), s32[]{:S(2)}) async-start(), calls=%async_computation.21 | async-start | bytes 5242880 | tf_op jit(solution)/shard_map/while/body/eval_jaxpr/reduce_scatter | solution.py:105
  2528.1 160.6 %reduce-scatter.34.cloned.1.call-start = ((), (), s32[]{:S(2)}) async-start(), calls=%async_computation.23 | async-start | bytes 5242880 | tf_op jit(solution)/shard_map/while/body/eval_jaxpr/reduce_scatter | solution.py:105
  2718.4 141.1 %reduce-scatter.20.cloned.1.call-start = ((), (), s32[]{:S(2)}) async-start(), calls=%async_computation.14 | async-start | bytes 2621440 | tf_op jit(solution)/shard_map/reduce_scatter | solution.py:315
  2722.4 171.1 %reduce-scatter.18.cloned.1.call-start = ((), (), s32[]{:S(2)}) async-start(), calls=%async_computation.13 | async-start | bytes 2621440 | tf_op jit(solution)/shard_map/reduce_scatter | solution.py:312
  (184 other events, 4474.9 us)
Sparse Core Ops, SparseCore 0:
  84.2 76.0 reduce-scatter.23
  214.6 75.8 reduce-scatter.25
  375.4 76.4 reduce-scatter.23
  506.1 75.8 reduce-scatter.25
  666.9 76.4 reduce-scatter.23
  797.6 75.8 reduce-scatter.25
  967.6 76.4 reduce-scatter.27
  1099.1 75.8 reduce-scatter.29
  1180.9 46.4 all-gather.2
  1241.2 75.4 reduce-scatter.31
  1321.7 46.4 all-gather.4
  1406.6 75.4 reduce-scatter.33
  1572.7 74.5 reduce-scatter.27
  1702.3 75.9 reduce-scatter.29
  1784.1 46.4 all-gather.2
  1844.4 75.4 reduce-scatter.31
  1924.9 46.4 all-gather.4
  2010.1 75.4 reduce-scatter.33
  2175.9 74.5 reduce-scatter.27
  2305.6 75.9 reduce-scatter.29
  2387.4 46.4 all-gather.2
  2447.7 75.4 reduce-scatter.31
  2528.2 46.4 all-gather.4
  2613.1 75.4 reduce-scatter.33
Sparse Core Ops, SparseCore 1:
  2715.7 55.4 reduce-scatter.21
  2774.3 20.5 reduce-scatter.15
  2797.3 28.1 reduce-scatter.13
  2828.2 31.3 reduce-scatter.19
  2862.1 31.3 reduce-scatter.17
